TPU v7x, 512 devices: a whole 4x4x16 slice. The times are simulated.
512 devices in a mesh: grp: 32 (over y, x, core), shard: 16 (over z).
Axes of the slice: x: 4, y: 4, z: 16, core: 2. Of those that a mesh axis runs over, the one named last changes fastest.
Arguments:
- grads: bfloat16 [2, 32, 16, 768, 768], P(None, 'grp', 'shard')
- vec_grads: bfloat16 [2, 32, 16, 8, 768], P(None, 'grp', 'shard'), may hold values from -0.5 to 0.5
- weight: float32 [768, 768], P('shard'), may hold values from -0.21875 to 0.21875
- basis: float32 [768, 256], replicated, may hold values from -0.21875 to 0.21875
- moment: float32 [768, 256], P('shard'), may hold values from -4 to 4
- second: float32 [768, 256], P('shard'), may hold values from 0.01 to 1
- vectors: float32 [8, 768], P(None, 'shard'), may hold values from -6 to 6
- vec_moment: float32 [8, 768], P(None, 'shard'), may hold values from -1.5 to 1.5
- vec_second: float32 [8, 768], P(None, 'shard'), may hold values from 0.001 to 0.1
Outputs:
- new_weight: float32 [768, 768], P('shard')
- update: bfloat16 [768, 768], P('shard')
- new_moment: float32 [768, 256], P('shard')
- new_second: float32 [768, 256], P('shard')
- new_basis: float32 [768, 256], replicated
- new_vectors: float32 [8, 768], P(None, 'shard')
- new_vec_moment: float32 [8, 768], P(None, 'shard')
- new_vec_second: float32 [8, 768], P(None, 'shard')
All inputs are finite; a program needn't handle non-finite values.
Results may differ from a plain program's by a relative error of at most 0.001.
Values sent between devices are 32-bit elements; how exact they have to be, the bound alone decides.
A program may use at most 64 MiB of HBM per device.

v0:
```python
import jax
import jax.numpy as jnp
from jax import lax
from jax.sharding import PartitionSpec as P

NS_STEPS = 5
STEP = 100
HIGH = lax.Precision.HIGHEST


def matmul(left, right):
    return jnp.dot(left, right, precision=HIGH, preferred_element_type=jnp.float32)


def per_device(grads, vec_grads, weight, basis, moment, second, vectors, vec_moment, vec_second):
    shards = lax.axis_size("shard")
    width = grads.shape[-1]
    rows = weight.shape[0]
    cols = vectors.shape[1]
    me = lax.axis_index("shard")
    summed = grads[0, 0, 0].astype(jnp.float32) + grads[1, 0, 0].astype(jnp.float32)
    vec_local = vec_grads[0, 0, 0].astype(jnp.float32) + vec_grads[1, 0, 0].astype(jnp.float32)
    packed = jnp.concatenate([summed, vec_local], axis=0)
    packed = lax.psum(packed, ("grp", "shard"))
    total = packed[:width]
    vec_total = packed[width:]
    projected_all = matmul(total, basis)
    subspace = lax.dot_general(
        total,
        projected_all,
        (((0,), (0,)), ((), ())),
        precision=HIGH,
        preferred_element_type=jnp.float32,
    )
    squares = jnp.sum(total * total) + jnp.sum(vec_total * vec_total)
    iterate = subspace / jnp.sqrt(jnp.sum(subspace * subspace) + 1e-06)
    for step in range(NS_STEPS):
        gram = matmul(iterate.T, iterate)
        iterate = 1.5 * iterate - 0.5 * matmul(iterate, gram)
    factor = 1.0 / jnp.maximum(jnp.sqrt(squares / (width * width + vec_total.size)), 1.0)
    projected = lax.dynamic_slice_in_dim(projected_all, me * rows, rows, axis=0)
    vec_sum = lax.dynamic_slice_in_dim(vec_total, me * cols, cols, axis=1)
    first_fix = 1.0 - 0.9**STEP
    second_fix = 1.0 - 0.999**STEP
    grad_low = factor * projected
    new_moment = 0.9 * moment + 0.1 * grad_low
    new_second = 0.999 * second + 0.001 * grad_low * grad_low
    normalized = new_moment / first_fix / (jnp.sqrt(new_second / second_fix) + 1e-08)
    full = lax.dot_general(
        normalized,
        basis,
        (((1,), (1,)), ((), ())),
        precision=HIGH,
        preferred_element_type=jnp.float32,
    )
    new_weight = weight - 0.001 * (0.25 * full + 0.01 * weight)
    vec_grad = factor * vec_sum
    new_vec_moment = 0.9 * vec_moment + 0.1 * vec_grad
    new_vec_second = 0.999 * vec_second + 0.001 * vec_grad * vec_grad
    vec_step = new_vec_moment / first_fix / (jnp.sqrt(new_vec_second / second_fix) + 1e-08)
    new_vectors = vectors - 0.001 * (vec_step + 0.01 * vectors)
    return (
        new_weight,
        full.astype(jnp.bfloat16),
        new_moment,
        new_second,
        iterate,
        new_vectors,
        new_vec_moment,
        new_vec_second,
    )


def solution(mesh):
    return jax.shard_map(
        per_device,
        mesh=mesh,
        in_specs=(
            P(None, "grp", "shard", None, None),
            P(None, "grp", "shard", None, None),
            P("shard", None),
            P(),
            P("shard", None),
            P("shard", None),
            P(None, "shard"),
            P(None, "shard"),
            P(None, "shard"),
        ),
        out_specs=(
            P("shard", None),
            P("shard", None),
            P("shard", None),
            P("shard", None),
            P(),
            P(None, "shard"),
            P(None, "shard"),
            P(None, "shard"),
        ),
        check_vma=False,
    )
```

profile of v0, /device:TPU:1, one launch (start us, length us, event | category | flops | bytes accessed | tf_op | source)
XLA Modules:
  0.0 534.5 jit_solution(420021904912794236)
XLA Ops:
  7.2 0.0 copy-start
  7.2 0.0 all-reduce.2.cloned.1.call-start
  7.2 0.8 add_bitcast_fusion.1
  8.0 1.9 add_bitcast_fusion
  9.9 1.6 pad_maximum_fusion
  11.5 0.0 all-reduce.2.cloned.1.call-update
  11.5 485.5 %all-reduce.2.cloned.1.call-done = f32[776,768]{1,0:T(8,128)} async-done(((f32[776,768]{1,0:T(8,128)}), f32[776,768]{1,0:T(8,128)}) %all-reduce.2.cloned.1.call-update) | async-done | bytes 2383888 | tf_op jit(solution)/shard_map/psum | solution.py:24
  497.0 0.0 copy-start.1
  497.0 3.0 multiply_reduce_fusion
  500.0 1.3 fusion.25
  502.7 0.0 copy-done
  502.7 0.0 copy-done.1
  502.7 2.0 fusion.2
  504.7 0.0 copy-start.2
  504.8 5.3 multiply_reduce_fusion.1
  510.1 0.0 copy-done.2
  510.1 0.0 copy-start.3
  510.9 2.9 fusion.9
  513.8 0.0 copy-done.3
  513.8 0.8 fusion.8
  514.6 1.4 fusion.27
  516.0 0.8 fusion.7
  516.8 1.6 fusion.28
  518.4 0.8 fusion.6
  519.2 1.4 fusion.29
  520.6 0.0 copy-start.7
  520.6 0.0 copy-start.8
  520.7 0.8 fusion.5
  521.4 0.0 copy-start.6
  521.5 0.0 copy-start.9
  521.5 0.0 copy-start.10
  521.5 0.0 copy-start.11
  521.5 1.4 fusion.30
  522.9 1.7 fusion.4
  524.6 0.0 copy-done.7
  524.6 0.0 copy-done.8
  524.6 0.8 multiply_add_fusion
  525.4 0.0 copy-start.4
  525.4 0.0 copy-start.5
  525.4 0.0 copy-done.6
  525.5 1.5 fusion.26
  527.0 0.0 copy-done.9
  527.0 0.0 copy-done.10
  527.0 0.0 copy-done.11
  527.0 0.7 multiply_subtract_fusion.1
  527.7 0.0 copy-done.4
  527.7 0.0 copy-done.5
Async XLA Ops:
  7.2 495.5 %copy-start = (f32[768,256]{1,0:T(8,128)S(1)}, f32[768,256]{1,0:T(8,128)}, u32[]{:S(2)}) copy-start(f32[768,256]{1,0:T(8,128)} %param.12) | copy-start | bytes 2359300
  7.2 489.8 %all-reduce.2.cloned.1.call-start = ((), (), s32[]{:S(2)}) async-start(), calls=%async_computation | async-start | bytes 4767744 | tf_op jit(solution)/shard_map/psum | solution.py:24
  497.0 5.8 %copy-start.1 = (f32[776,768]{1,0:T(8,128)S(1)}, f32[776,768]{1,0:T(8,128)}, u32[]{:S(2)}) copy-start(f32[776,768]{1,0:T(8,128)} %all-reduce.2.cloned.1.call-done) | copy-start | bytes 7151620
  504.7 5.3 %copy-start.2 = (f32[768,256]{1,0:T(8,128)}, f32[768,256]{1,0:T(8,128)S(1)}, u32[]{:S(2)}) copy-start(f32[768,256]{1,0:T(8,128)S(1)} %fusion.2) | copy-start | bytes 2359300
  510.1 3.7 copy-start.3
  520.6 4.0 copy-start.7
  520.6 4.0 copy-start.8
  521.4 4.0 copy-start.6
  521.5 5.5 %copy-start.9 = (f32[8,48]{1,0:T(8,128)S(1)}, f32[8,48]{1,0:T(8,128)}, u32[]{:S(2)}) copy-start(f32[8,48]{1,0:T(8,128)} %param.15) | copy-start | bytes 4612
  521.5 5.5 %copy-start.10 = (f32[8,48]{1,0:T(8,128)S(1)}, f32[8,48]{1,0:T(8,128)}, u32[]{:S(2)}) copy-start(f32[8,48]{1,0:T(8,128)} %param.16) | copy-start | bytes 4612
  521.5 5.5 %copy-start.11 = (f32[8,48]{1,0:T(8,128)S(1)}, f32[8,48]{1,0:T(8,128)}, u32[]{:S(2)}) copy-start(f32[8,48]{1,0:T(8,128)} %param.17) | copy-start | bytes 4612
  525.4 2.3 copy-start.4
  525.4 2.3 copy-start.5
Sparse Core Ops, SparseCore 0:
  13.4 483.5 all-reduce.1
where the time goes:
time: 535 us
  waiting for transfers between devices  485 us (91%)
  matrix products  22.4 us (4%)
  between operations  16.4 us (3%)
  other arithmetic  10.1 us (2%)
    psum x1, waiting for transfers between devices, per_device(): packed = lax.psum(packed, ('grp', 'shard'))  485 us
    dot_general x11, matrix products, matmul(): jnp.dot(left, right, precision=HIGH, preferred_element_type=jnp.float32)  15.6 us
  transfers between devices with their start and end apart: 1, of which 1 were waited for; matrix products, arithmetic and copies ran while one was open for 0% of the time, Pallas kernels for 0%

commit v1 on v0

--- a/solution.py
+++ b/solution.py
@@ -6,6 +6,11 @@
 NS_STEPS = 5
 STEP = 100
 HIGH = lax.Precision.HIGHEST
+
+
+def one_after_other(array, first, second_2):
+    partial = lax.psum(array, first)
+    return lax.psum(partial, second_2)
 
 
 def matmul(left, right):
@@ -21,7 +26,7 @@
     summed = grads[0, 0, 0].astype(jnp.float32) + grads[1, 0, 0].astype(jnp.float32)
     vec_local = vec_grads[0, 0, 0].astype(jnp.float32) + vec_grads[1, 0, 0].astype(jnp.float32)
     packed = jnp.concatenate([summed, vec_local], axis=0)
-    packed = lax.psum(packed, ("grp", "shard"))
+    packed = one_after_other(packed, "shard", "grp")
     total = packed[:width]
     vec_total = packed[width:]
     projected_all = matmul(total, basis)

time: 535 us -> 339 us (0.63)
  waiting for transfers between devices: 485 us -> 290 us
    psum x1 -> x2, waiting for transfers between devices: 485 us -> 290 us  [the longest x1 147 us: one_after_other(): return lax.psum(partial, second_2)]
  transfers between devices with their start and end apart: 1 -> 2, of which waited for: 1 -> 2; matrix products, arithmetic and copies ran while one was open for 0% -> 0% of each run, Pallas kernels for 0% -> 0%
where the time goes in v1:
time: 339 us
  waiting for transfers between devices  290 us (86%)
  matrix products  22.4 us (7%)
  between operations  16.4 us (5%)
  other arithmetic  10.1 us (3%)
    psum x1, waiting for transfers between devices, one_after_other(): return lax.psum(partial, second_2)  147 us
    psum x1, waiting for transfers between devices, one_after_other(): partial = lax.psum(array, first)  143 us
    dot_general x11, matrix products, matmul(): jnp.dot(left, right, precision=HIGH, preferred_element_type=jnp.float32)  15.6 us
  transfers between devices with their start and end apart: 2, of which 2 were waited for; matrix products, arithmetic and copies ran while one was open for 0% of the time, Pallas kernels for 0%

profile of v1, /device:TPU:1, one launch (start us, length us, event | category | flops | bytes accessed | tf_op | source)
XLA Modules:
  0.0 338.9 jit_solution(4495519119121037532)
XLA Ops:
  7.2 0.0 copy-start
  7.2 0.0 all-reduce.3.cloned.1.call-start
  7.2 0.8 add_bitcast_fusion.1
  8.0 1.9 add_bitcast_fusion
  9.9 1.6 pad_maximum_fusion
  11.5 0.0 all-reduce.3.cloned.1.call-update
  11.5 0.0 all-reduce.5.cloned.1.call-start
  11.5 143.2 %all-reduce.3.cloned.1.call-done = f32[776,768]{1,0:T(8,128)} async-done(((f32[776,768]{1,0:T(8,128)}), f32[776,768]{1,0:T(8,128)}) %all-reduce.3.cloned.1.call-update) | async-done | bytes 2383888 | tf_op jit(solution)/shard_map/psum | solution.py:12
  154.7 0.0 all-reduce.5.cloned.1.call-update
  154.7 146.6 %all-reduce.5.cloned.1.call-done = f32[776,768]{1,0:T(8,128)} async-done(((f32[776,768]{1,0:T(8,128)}), f32[776,768]{1,0:T(8,128)}) %all-reduce.5.cloned.1.call-update) | async-done | bytes 2383888 | tf_op jit(solution)/shard_map/psum | solution.py:13
  301.3 3.0 multiply_reduce_fusion
  304.4 1.3 fusion.25
  307.1 0.0 copy-done
  307.1 0.0 copy-done.1
  307.1 2.0 fusion.2
  309.1 0.0 copy-start.2
  309.1 5.3 %multiply_reduce_fusion.1 = (f32[]{:T(128)}, f32[768,256]{1,0:T(8,128)}) fusion(f32[768,256]{1,0:T(8,128)S(1)} %fusion.2, f32[776,768]{1,0:T(8,128)S(1)} %copy-done.1), kind=kOutput, calls=%fused_computation.17 | convolution fusion | flops 1812332544 | bytes 3932164 | tf_op jit(solution)/shard_map/dot_general | solution.py:33
  314.5 0.0 copy-done.2
  315.2 2.9 fusion.9
  318.1 0.0 copy-done.3
  318.2 0.8 fusion.8
  319.0 1.4 fusion.27
  320.4 0.8 fusion.7
  321.2 1.6 fusion.28
  322.8 0.8 fusion.6
  323.6 1.4 fusion.29
  325.0 0.0 copy-start.7
  325.0 0.0 copy-start.8
  325.0 0.8 fusion.5
  325.8 0.0 copy-start.6
  325.8 0.0 copy-start.9
  325.9 0.0 copy-start.10
  325.9 0.0 copy-start.11
  325.9 1.4 fusion.30
  327.3 1.7 fusion.4
  329.0 0.0 copy-done.7
  329.0 0.0 copy-done.8
  329.0 0.8 multiply_add_fusion
  329.8 0.0 copy-start.4
  329.8 0.0 copy-start.5
  329.8 0.0 copy-done.6
  329.8 1.5 fusion.26
  331.4 0.0 copy-done.9
  331.4 0.0 copy-done.10
  331.4 0.0 copy-done.11
  331.4 0.7 multiply_subtract_fusion.1
  332.1 0.0 copy-done.4
  332.1 0.0 copy-done.5
  (2 shorter events, 0.0 us)
Async XLA Ops:
  7.2 299.9 %copy-start = (f32[768,256]{1,0:T(8,128)S(1)}, f32[768,256]{1,0:T(8,128)}, u32[]{:S(2)}) copy-start(f32[768,256]{1,0:T(8,128)} %param.12) | copy-start | bytes 2359300
  7.2 147.5 %all-reduce.3.cloned.1.call-start = ((), (), s32[]{:S(2)}) async-start(), calls=%async_computation | async-start | bytes 4767744 | tf_op jit(solution)/shard_map/psum | solution.py:12
  11.5 289.9 %all-reduce.5.cloned.1.call-start = ((), (), s32[]{:S(2)}) async-start(), calls=%async_computation.1 | async-start | bytes 4767744 | tf_op jit(solution)/shard_map/psum | solution.py:13
  301.3 5.8 %copy-start.1 = (f32[776,768]{1,0:T(8,128)S(1)}, f32[776,768]{1,0:T(8,128)}, u32[]{:S(2)}) copy-start(f32[776,768]{1,0:T(8,128)} %all-reduce.5.cloned.1.call-done) | copy-start | bytes 7151620
  309.1 5.3 %copy-start.2 = (f32[768,256]{1,0:T(8,128)}, f32[768,256]{1,0:T(8,128)S(1)}, u32[]{:S(2)}) copy-start(f32[768,256]{1,0:T(8,128)S(1)} %fusion.2) | copy-start | bytes 2359300
  314.5 3.7 %copy-start.3 = (f32[768,256]{1,0:T(8,128)S(1)}, f32[768,256]{1,0:T(8,128)}, u32[]{:S(2)}) copy-start(f32[768,256]{1,0:T(8,128)} %get-tuple-element.18) | copy-start | bytes 2359300
  325.0 4.0 %copy-start.7 = (f32[48,256]{1,0:T(8,128)S(1)}, f32[48,256]{1,0:T(8,128)}, u32[]{:S(2)}) copy-start(f32[48,256]{1,0:T(8,128)} %param.13) | copy-start | bytes 147460
  325.0 4.0 %copy-start.8 = (f32[48,256]{1,0:T(8,128)S(1)}, f32[48,256]{1,0:T(8,128)}, u32[]{:S(2)}) copy-start(f32[48,256]{1,0:T(8,128)} %param.14) | copy-start | bytes 147460
  325.8 4.0 %copy-start.6 = (f32[48,768]{1,0:T(8,128)S(1)}, f32[48,768]{1,0:T(8,128)}, u32[]{:S(2)}) copy-start(f32[48,768]{1,0:T(8,128)} %param.11) | copy-start | bytes 442372
  325.8 5.5 %copy-start.9 = (f32[8,48]{1,0:T(8,128)S(1)}, f32[8,48]{1,0:T(8,128)}, u32[]{:S(2)}) copy-start(f32[8,48]{1,0:T(8,128)} %param.15) | copy-start | bytes 4612
  325.9 5.5 %copy-start.10 = (f32[8,48]{1,0:T(8,128)S(1)}, f32[8,48]{1,0:T(8,128)}, u32[]{:S(2)}) copy-start(f32[8,48]{1,0:T(8,128)} %param.16) | copy-start | bytes 4612
  325.9 5.5 %copy-start.11 = (f32[8,48]{1,0:T(8,128)S(1)}, f32[8,48]{1,0:T(8,128)}, u32[]{:S(2)}) copy-start(f32[8,48]{1,0:T(8,128)} %param.17) | copy-start | bytes 4612
  329.8 2.3 copy-start.4
  329.8 2.3 copy-start.5
Sparse Core Ops, SparseCore 0:
  11.6 143.0 all-reduce.2
  158.0 143.2 all-reduce.4
